TPU v7x, 512 devices: a whole 4x4x16 slice. The times are simulated.
512 devices in a mesh: ctx: 32 (over z, y_lo), exp: 8 (over x, core), dp: 2 (over y_hi).
Axes of the slice: x: 4, y: 4 (y_hi: 2, y_lo: 2; y = y_hi * 2 + y_lo), z: 16, core: 2. Of those that a mesh axis runs over, the one named last changes fastest.
Arguments:
- hidden_in: bfloat16 [2, 32768, 1024], P('dp', ('ctx', 'exp')), may hold values from -6 to 6
- queries: bfloat16 [2, 32768, 1024], P('dp', ('ctx', 'exp')), may hold values from -6 to 6
- keys: bfloat16 [2, 32768, 1024], P('dp', ('ctx', 'exp')), may hold values from -6 to 6
- values: bfloat16 [2, 32768, 1024], P('dp', ('ctx', 'exp')), may hold values from -6 to 6
- log_decay: float32 [2, 32768, 8], P('dp', ('ctx', 'exp')), may hold values from -1 to 0
- retention_gain: float32 [1024], replicated, may hold values from 0.25 to 1.75
- norm_gain: float32 [1024], replicated, may hold values from 0.25 to 1.75
- routes: int32 [2, 32768, 2], P('dp', ('ctx', 'exp')), may hold values from 0 to 63, all different within a row; in each aligned block of 128 rows (0 to 127, 128 to 255, ..., all dimensions but the last counted through in order) at most 5 rows name the same one
- route_weights: float32 [2, 32768, 2], P('dp', ('ctx', 'exp')), may hold values from 0.1 to 1
- w_gate: bfloat16 [64, 1024, 1408], P(('ctx', 'dp'), 'exp'), may hold values from -0.1875 to 0.1875
- w_up: bfloat16 [64, 1024, 1408], P(('ctx', 'dp'), 'exp'), may hold values from -0.1875 to 0.1875
- w_down: bfloat16 [64, 1024, 1408], P(('ctx', 'dp'), 'exp'), may hold values from -0.15625 to 0.15625
Outputs:
- output: bfloat16 [2, 32768, 1024], P('dp', ('ctx', 'exp'))
Inputs may be any that keep to these rules, and one draw needn't show every extreme that they name: `routes`: in each aligned block of 128 positions (the positions of one device) no expert is named more than 5 times, and a position's 2 experts differ.
All inputs are finite; a program needn't handle non-finite values.
Results may differ from a plain program's by a relative error of at most 0.007.
Values may be sent and summed in bfloat16 or wider, within the bound.
No kernel may reach another device: no remote copies, remote signals or barrier semaphores. Data moves between devices by JAX's collectives and lax.ppermute only.
A program may use at most 128 MiB of HBM per device.

v0:
```python
import jax
import jax.numpy as jnp
from jax import lax
from jax.sharding import Mesh, PartitionSpec as P

CTX = ("z", "ylo")
EXP = ("x", "core")
OWNERS = ("z", "ylo", "yhi")


def exchange(blocks, axes):
    return lax.all_to_all(blocks, axes, split_axis=0, concat_axis=0, tiled=True)


def rotate(vectors, token_position):
    half_dim = vectors.shape[-1] // 2
    inverse = 10000.0 ** (-jnp.arange(half_dim, dtype=jnp.float32) / half_dim)
    angles = token_position.astype(jnp.float32)[:, None] * inverse[None, :]
    cosine = jnp.cos(angles)[:, None, :]
    sine_part = jnp.sin(angles)[:, None, :]
    leading = vectors[..., :half_dim]
    trailing = vectors[..., half_dim:]
    return jnp.concatenate(
        [leading * cosine - trailing * sine_part, trailing * cosine + leading * sine_part], axis=-1
    )


def entering_state(block_summary, block_log):
    member_count = lax.axis_size(EXP)
    ctx_count = lax.axis_size(CTX)
    own_head = lax.axis_index(EXP)
    own_ctx = lax.axis_index(CTX)
    all_logs = lax.all_gather(block_log, CTX + EXP, axis=0).reshape(ctx_count, member_count, -1)
    head_logs = lax.dynamic_index_in_dim(all_logs, own_head, 2, keepdims=False)
    group_logs = jnp.sum(head_logs, axis=1)
    own_logs = lax.dynamic_index_in_dim(head_logs, own_ctx, 0, keepdims=False)
    members = jnp.arange(member_count)
    ctxs = jnp.arange(ctx_count)
    summaries = exchange(block_summary.astype(jnp.bfloat16), EXP).astype(jnp.float32)
    after = jnp.exp(
        jnp.sum(jnp.where(members[None, :] > members[:, None], own_logs[None, :], 0.0), 1)
    )
    group_sum = jnp.sum(after[:, None, None] * summaries, axis=0)
    group_sums = lax.all_gather(group_sum.astype(jnp.bfloat16), CTX, axis=0).astype(jnp.float32)
    between = (ctxs[None, :] > ctxs[:, None]) & (ctxs[None, :] < own_ctx)
    reach = jnp.exp(jnp.sum(jnp.where(between, group_logs[None, :], 0.0), 1))
    reach = jnp.where(ctxs < own_ctx, reach, 0.0)
    leading = jnp.sum(reach[:, None, None] * group_sums, axis=0)
    to_block = jnp.exp(
        jnp.sum(jnp.where(members[None, :] < members[:, None], own_logs[None, :], 0.0), 1)
    )
    inner = (members[None, None, :] > members[None, :, None]) & (
        members[None, None, :] < members[:, None, None]
    )
    inner = jnp.exp(jnp.sum(jnp.where(inner, own_logs[None, None, :], 0.0), 2))
    inner = jnp.where(members[None, :] < members[:, None], inner, 0.0)
    entering = to_block[:, None, None] * leading[None] + jnp.sum(
        inner[:, :, None, None] * summaries[None], axis=1
    )
    return exchange(entering.astype(jnp.bfloat16), EXP)


def body(
    hidden_in,
    queries,
    keys,
    values,
    log_decay,
    retention_gain,
    norm_gain,
    routes,
    route_weights,
    w_gate,
    w_up,
    w_down,
):
    tok_rows = hidden_in.shape[1]
    model_width = hidden_in.shape[2]
    head_count = log_decay.shape[2]
    head_dim = model_width // head_count
    block_index = lax.axis_index(CTX) * lax.axis_size(EXP) + lax.axis_index(EXP)
    token_position = block_index * tok_rows + jnp.arange(tok_rows, dtype=jnp.int32)
    per_head_keys = rotate(
        keys[0].astype(jnp.float32).reshape(tok_rows, head_count, head_dim), token_position
    ).astype(jnp.bfloat16)
    per_head_values = values[0].reshape(tok_rows, head_count, head_dim)
    running_total = jnp.cumsum(log_decay[0], axis=0)
    trailing_decay = jnp.exp(running_total[-1][None, :] - running_total)
    block_summary = jnp.einsum(
        "qpf,qpy->pfy",
        per_head_keys.astype(jnp.float32) * trailing_decay[:, :, None],
        per_head_values.astype(jnp.float32),
        precision=lax.Precision.HIGHEST,
    )
    state_in = entering_state(block_summary, running_total[-1])
    per_head_queries = (
        rotate(
            queries[0].astype(jnp.float32).reshape(tok_rows, head_count, head_dim), token_position
        )
        * head_dim ** (-0.5)
    ).astype(jnp.bfloat16)
    scores = jnp.einsum(
        "thd,shd->hts", per_head_queries, per_head_keys, preferred_element_type=jnp.float32
    )
    causal = jnp.arange(tok_rows)[:, None] >= jnp.arange(tok_rows)[None, :]
    spread = running_total.T[:, :, None] - running_total.T[:, None, :]
    weights = jnp.where(
        causal[None], scores * jnp.exp(jnp.where(causal[None], spread, 0.0)), 0.0
    ).astype(jnp.bfloat16)
    inside = jnp.einsum(
        "hts,shd->thd", weights, per_head_values, preferred_element_type=jnp.float32
    )
    external_part = jnp.exp(running_total)[:, :, None] * jnp.einsum(
        "wjc,jco->wjo", per_head_queries, state_in, preferred_element_type=jnp.float32
    )
    retrieved = inside + external_part
    centre = jnp.mean(retrieved, axis=-1, keepdims=True)
    deviation = retrieved - centre
    variance = jnp.mean(deviation * deviation, axis=-1, keepdims=True)
    normalized = (deviation * lax.rsqrt(variance + 1e-05)).reshape(tok_rows, model_width)
    residual = hidden_in[0].astype(jnp.float32) + retention_gain * normalized
    square_mean = jnp.mean(residual * residual, axis=-1, keepdims=True)
    normed = (residual * lax.rsqrt(square_mean + 1e-06) * norm_gain).astype(jnp.bfloat16)
    expert_count = lax.axis_size(OWNERS)
    top_count = routes.shape[2]
    capacity = (tok_rows * top_count * 5 + 4 * expert_count - 1) // (4 * expert_count)
    slot_count = expert_count * capacity
    route_rows = routes[0]
    expert_hits = (
        route_rows.reshape(tok_rows * top_count)[:, None]
        == jnp.arange(expert_count, dtype=jnp.int32)[None, :]
    ).astype(jnp.int32)
    earlier = jnp.cumsum(expert_hits, axis=0) - expert_hits
    slot_rank = jnp.sum(earlier * expert_hits, axis=1).reshape(tok_rows, top_count)
    destination = route_rows * capacity + slot_rank
    slot_lanes = jnp.arange(slot_count, dtype=jnp.int32)
    placing = jnp.any(destination[None, :, :] == slot_lanes[:, None, None], axis=2).astype(
        jnp.bfloat16
    )
    outgoing = jnp.dot(placing, normed, preferred_element_type=jnp.float32).astype(jnp.bfloat16)
    lanes = 128
    packed = (expert_count, capacity * model_width // lanes, lanes)
    arrived = exchange(outgoing.reshape(packed), OWNERS).reshape(slot_count, model_width)
    gate_full = lax.all_gather(w_gate[0], EXP, axis=0, tiled=True)
    up_full = lax.all_gather(w_up[0], EXP, axis=0, tiled=True)
    down_full = lax.all_gather(w_down[0], EXP, axis=0, tiled=True)
    gate_next = jnp.dot(arrived, gate_full, preferred_element_type=jnp.float32)
    up_next = jnp.dot(arrived, up_full, preferred_element_type=jnp.float32)
    hidden = (jax.nn.silu(gate_next) * up_next).astype(jnp.bfloat16)
    expert_out = lax.dot_general(
        hidden, down_full, (((1,), (1,)), ((), ())), preferred_element_type=jnp.float32
    ).astype(jnp.bfloat16)
    returned = exchange(expert_out.reshape(packed), OWNERS).reshape(slot_count, model_width)
    output = residual
    for route_index in range(top_count):
        picking = (destination[:, route_index][:, None] == slot_lanes[None, :]).astype(jnp.bfloat16)
        routed = jnp.dot(picking, returned, preferred_element_type=jnp.float32)
        output = output + route_weights[0][:, route_index][:, None] * routed
    return output.astype(jnp.bfloat16)[None]


def solution(mesh):
    ctx, exp, dp = (mesh.shape["ctx"], mesh.shape["exp"], mesh.shape["dp"])
    split = Mesh(
        mesh.devices.reshape(ctx // 2, 2, exp // 2, 2, dp), ("z", "ylo", "x", "core", "yhi")
    )
    tokens = P("yhi", CTX + EXP, None)
    experts = P(OWNERS, EXP, None)
    in_specs = (tokens,) * 5 + (P(), P()) + (tokens,) * 2 + (experts,) * 3
    return jax.shard_map(body, mesh=split, in_specs=in_specs, out_specs=tokens, check_vma=False)
```

profile of v0, /device:TPU:8, one launch (start us, length us, event | category | flops | bytes accessed | tf_op | source)
XLA Modules:
  0.0 633.6 jit_solution(9688745371011176003)
XLA Ops:
  6.6 1.2 copy.84
  9.2 1.0 copy.114
  10.2 0.3 multiply_cosine_fusion
  10.6 0.3 multiply_subtract_fusion
  10.9 0.7 copy-done.1
  11.7 1.5 convolution_convert_fusion.1
  13.2 4.3 all-to-all-start
  17.6 305.4 %all-gather.4 = f32[256,1,8]{2,1,0:T(1,128)S(1)} all-gather(f32[1,1,8]{2,1,0:T(1,128)S(1)} %get-tuple-element.21), channel_id=1, replica_groups=mesh['z'=16,'ylo'=2,'x'=4,'core'=2,'yhi'=2] {'z','ylo','x','core'}, dimensions={0}, use_global_device_ids=true | all-gather | bytes 8224 | tf_op jit(solution)/shard_map/all_gather | solution.py:33
  323.3 0.7 multiply_reduce_fusion.3
  324.1 0.7 all-gather.12.cloned.1.call-update
  324.9 0.7 all-gather.14.cloned.1.call-update
  325.6 0.5 all-gather.16.cloned.1.call-update
  326.2 0.5 dynamic-slice_reduce_fusion
  327.3 0.6 reduce-window.6
  328.6 0.6 multiply_reduce_fusion
  329.4 125.0 %all-gather.10.cloned.1.call-done = bf16[4096,128]{1,0:T(8,128)(2,1)} async-done(((bf16[128,128]{1,0:T(8,128)(2,1)}), bf16[4096,128]{1,0:T(8,128)(2,1)}) %all-gather.10.cloned.1.call-update) | async-done | bytes 1048592 | tf_op jit(solution)/shard_map/all_gather | solution.py:44
  454.4 1.5 fusion.8
  456.0 0.8 add_convert_fusion
  456.9 4.2 all-to-all-start.1
  461.4 7.1 %all-to-all-done.1 = bf16[8,128,128]{1,2,0:T(8,128)(2,1)S(1)} async-done(((bf16[8,128,128]{1,2,0:T(8,128)(2,1)}), bf16[8,128,128]{1,2,0:T(8,128)(2,1)S(1)}, u32[]{:S(2)}, u32[]{:S(2)}) %all-to-all-start.1) | async-done | bytes 262176 | tf_op jit(solution)/shard_map/all_to_all | solution.py:12
  468.6 0.3 fusion.13
  468.9 0.6 fusion.53
  470.2 0.4 convolution_convert_fusion
  470.9 52.5 %all_to_all.20 = bf16[64,40,128]{2,1,0:T(8,128)(2,1)S(1)} all-to-all(bf16[64,40,128]{2,1,0:T(8,128)(2,1)S(1)} %reshape.252), channel_id=1, replica_groups=mesh['z'=16,'ylo'=2,'x'=4,'core'=2,'yhi'=2] {'z','ylo','yhi'}, dimensions={0} | all-to-all | bytes 1310720 | tf_op jit(solution)/shard_map/all_to_all | solution.py:12
  523.7 4.3 fusion.3
  528.0 36.3 %all-gather.16.cloned.1.call-done = bf16[1,1024,1408]{2,1,0:T(8,128)(2,1)} async-done(((bf16[1,128,1408]{2,1,0:T(8,128)(2,1)}), bf16[1,1024,1408]{2,1,0:T(8,128)(2,1)}) %all-gather.16.cloned.1.call-update) | async-done | bytes 2883600 | tf_op jit(solution)/shard_map/all_gather | solution.py:146
  564.3 5.4 fusion.9
  569.8 1.1 reshape.254
  570.9 15.7 %all-to-all-start.3 = ((bf16[64,40,128]{2,1,0:T(8,128)(2,1)}), bf16[64,40,128]{2,1,0:T(8,128)(2,1)S(1)}, u32[]{:S(2)}, u32[]{:S(2)}) async-start(bf16[64,40,128]{2,1,0:T(8,128)(2,1)} %reshape.254), calls=%async_computation.3 | async-start | bytes 1310720 | tf_op jit(solution)/shard_map/all_to_all | solution.py:12
  587.0 38.4 %all-to-all-done.3 = bf16[64,40,128]{2,1,0:T(8,128)(2,1)S(1)} async-done(((bf16[64,40,128]{2,1,0:T(8,128)(2,1)}), bf16[64,40,128]{2,1,0:T(8,128)(2,1)S(1)}, u32[]{:S(2)}, u32[]{:S(2)}) %all-to-all-start.3) | async-done | bytes 655392 | tf_op jit(solution)/shard_map/all_to_all | solution.py:12
  625.7 0.4 fusion.16
  626.0 1.1 fusion.19
  (87 shorter events, 5.8 us)
Async XLA Ops:
  6.5 1.7 copy-start.5
  8.0 0.9 copy-start.8
  10.9 0.7 copy-start.1
  10.9 0.8 copy-start.3
  10.9 315.8 %copy-start.9 = (s32[1,128,2]{1,2,0:T(2,128)S(1)}, s32[1,128,2]{1,2,0:T(2,128)}, u32[]{:S(2)}) copy-start(s32[1,128,2]{1,2,0:T(2,128)} %param.19) | copy-start | bytes 3076
  13.2 310.1 %all-to-all-start = ((bf16[8,128,128]{2,1,0:T(8,128)(2,1)}), bf16[8,128,128]{2,1,0:T(8,128)(2,1)S(1)}, u32[]{:S(2)}, u32[]{:S(2)}) async-start(bf16[8,128,128]{2,1,0:T(8,128)(2,1)} %convolution_convert_fusion.1), calls=%async_computation | async-start | bytes 524288 | tf_op jit(solution)/shard_map/all_to_all | solution.py:12
  17.5 436.9 %all-gather.10.cloned.1.call-start = ((), (), s32[]{:S(2)}) async-start(), calls=%async_computation.4 | async-start | bytes 1081344 | tf_op jit(solution)/shard_map/all_gather | solution.py:44
  324.1 199.6 %all-gather.12.cloned.1.call-start = ((), (), s32[]{:S(2)}) async-start(), calls=%async_computation.5 | async-start | bytes 3244032 | tf_op jit(solution)/shard_map/all_gather | solution.py:144
  324.8 203.2 %all-gather.14.cloned.1.call-start = ((), (), s32[]{:S(2)}) async-start(), calls=%async_computation.6 | async-start | bytes 3244032 | tf_op jit(solution)/shard_map/all_gather | solution.py:145
  325.6 238.7 %all-gather.16.cloned.1.call-start = ((), (), s32[]{:S(2)}) async-start(), calls=%async_computation.7 | async-start | bytes 3244032 | tf_op jit(solution)/shard_map/all_gather | solution.py:146
  455.9 12.9 %copy-start.2 = (bf16[128,8,64]{2,0,1:T(8,128)(2,1)S(1)}, bf16[128,8,64]{2,0,1:T(8,128)(2,1)}, u32[]{:S(2)}) copy-start(bf16[128,8,64]{2,0,1:T(8,128)(2,1)} %copy-done.1) | copy-start | bytes 393220
  455.9 12.9 %copy-start.4 = (bf16[128,8,64]{2,0,1:T(8,128)(2,1)S(1)}, bf16[128,8,64]{2,0,1:T(8,128)(2,1)}, u32[]{:S(2)}) copy-start(bf16[128,8,64]{2,0,1:T(8,128)(2,1)} %copy-done.3) | copy-start | bytes 393220
  456.9 11.7 %all-to-all-start.1 = ((bf16[8,128,128]{1,2,0:T(8,128)(2,1)}), bf16[8,128,128]{1,2,0:T(8,128)(2,1)S(1)}, u32[]{:S(2)}, u32[]{:S(2)}) async-start(bf16[8,128,128]{1,2,0:T(8,128)(2,1)} %add_convert_fusion), calls=%async_computation.1 | async-start | bytes 524288 | tf_op jit(solution)/shard_map/all_to_all | solution.py:12
  468.9 1.0 copy-start
  468.9 1.0 copy-start.6
  469.5 0.7 copy-start.7
  569.8 17.2 %copy-start.10 = (f32[1,128,2]{1,2,0:T(2,128)S(1)}, f32[1,128,2]{1,2,0:T(2,128)}, u32[]{:S(2)}) copy-start(f32[1,128,2]{1,2,0:T(2,128)} %param.20) | copy-start | bytes 3076
  570.9 54.5 %all-to-all-start.3 = ((bf16[64,40,128]{2,1,0:T(8,128)(2,1)}), bf16[64,40,128]{2,1,0:T(8,128)(2,1)S(1)}, u32[]{:S(2)}, u32[]{:S(2)}) async-start(bf16[64,40,128]{2,1,0:T(8,128)(2,1)} %reshape.254), calls=%async_computation.3 | async-start | bytes 1310720 | tf_op jit(solution)/shard_map/all_to_all | solution.py:12
Sparse Core Ops, SparseCore 0:
  324.2 130.1 all-gather.9
  456.5 34.1 all-gather.11
  492.9 34.6 all-gather.13
  529.6 34.6 all-gather.15
where the time goes:
time: 634 us
  blocking collectives  358 us (56%)
  waiting for transfers between devices  209 us (33%)
  starting transfers between devices  24.4 us (4%)
  matrix products  14 us (2%)
  between operations  13.6 us (2%)
  local copies, waits for them, and re-layouts  8.17 us (1%)
  other arithmetic  6.77 us (1%)
    all_gather x1, blocking collectives, entering_state(): lax.all_gather(block_log, CTX + EXP, axis=0)  305 us
    all_gather x1, waiting for transfers between devices, entering_state(): lax.all_gather(group_sum.astype(jnp.bfloat16), CTX, axis=0)  125 us
    all_to_all x1, blocking collectives, exchange(): return lax.all_to_all(blocks, axes, split_axis=0, concat_axis=0, tiled=True)  52.5 us
    all_to_all x3, waiting for transfers between devices, exchange(): return lax.all_to_all(blocks, axes, split_axis=0, concat_axis=0, tiled=True)  45.5 us
    all_gather x1, waiting for transfers between devices, body(): down_full = lax.all_gather(w_down[0], EXP, axis=0, tiled=True)  36.3 us
    all_to_all x3, starting transfers between devices, exchange(): return lax.all_to_all(blocks, axes, split_axis=0, concat_axis=0, tiled=True)  24.2 us
  transfers between devices with their start and end apart: 7, of which 4 were waited for; matrix products, arithmetic and copies ran while one was open for 2% of the time, Pallas kernels for 0%

commit v1 on v0

--- a/solution.py
+++ b/solution.py
@@ -143,7 +143,11 @@
     arrived = exchange(outgoing.reshape(packed), OWNERS).reshape(slot_count, model_width)
     gate_full = lax.all_gather(w_gate[0], EXP, axis=0, tiled=True)
     up_full = lax.all_gather(w_up[0], EXP, axis=0, tiled=True)
-    down_full = lax.all_gather(w_down[0], EXP, axis=0, tiled=True)
+    block = w_down[0]
+    size = lax.axis_size(EXP)
+    pieces = jnp.stack([block for _ in range(size)])
+    pieces = lax.all_to_all(pieces, EXP, split_axis=0, concat_axis=0)
+    down_full = jnp.concatenate(pieces, axis=0)
     gate_next = jnp.dot(arrived, gate_full, preferred_element_type=jnp.float32)
     up_next = jnp.dot(arrived, up_full, preferred_element_type=jnp.float32)
     hidden = (jax.nn.silu(gate_next) * up_next).astype(jnp.bfloat16)

time: 634 us -> 629 us (level)
  blocking collectives: 358 us -> 305 us
  waiting for transfers between devices: 209 us -> 239 us
  starting transfers between devices: 24.4 us -> 34.5 us
    all_to_all x1 -> x0, blocking collectives: 52.5 us -> none  [exchange(): return lax.all_to_all(blocks, axes, split_axis=0, concat_axis=0, tiled=True)]
    all_to_all x3 -> x4, waiting for transfers between devices: 45.5 us -> 83.3 us  [exchange(): return lax.all_to_all(blocks, axes, split_axis=0, concat_axis=0, tiled=True)]
    all_gather x1 -> x0, waiting for transfers between devices: 36.3 us -> none  [body(): down_full = lax.all_gather(w_down[0], EXP, axis=0, tiled=True)]
    all_to_all x0 -> x1, waiting for transfers between devices: none -> 28.7 us  [body(): pieces = lax.all_to_all(pieces, EXP, split_axis=0, concat_axis=0)]
    all_to_all x3 -> x4, starting transfers between devices: 24.2 us -> 30.5 us  [exchange(): return lax.all_to_all(blocks, axes, split_axis=0, concat_axis=0, tiled=True)]
  transfers between devices with their start and end apart: 7 -> 8, of which waited for: 4 -> 5; matrix products, arithmetic and copies ran while one was open for 2% -> 3% of each run, Pallas kernels for 0% -> 0%
where the time goes in v1:
time: 629 us; the launch traced here: 628 us
  blocking collectives  305 us (48%)
  waiting for transfers between devices  239 us (38%)
  starting transfers between devices  34.5 us (5%)
  local copies, waits for them, and re-layouts  14.4 us (2%)
  matrix products  14.3 us (2%)
  between operations  13.6 us (2%)
  other arithmetic  7.36 us (1%)
    all_gather x1, blocking collectives, entering_state(): lax.all_gather(block_log, CTX + EXP, axis=0)  305 us
    all_gather x1, waiting for transfers between devices, entering_state(): lax.all_gather(group_sum.astype(jnp.bfloat16), CTX, axis=0)  125 us
    all_to_all x4, waiting for transfers between devices, exchange(): return lax.all_to_all(blocks, axes, split_axis=0, concat_axis=0, tiled=True)  83.3 us
    all_to_all x4, starting transfers between devices, exchange(): return lax.all_to_all(blocks, axes, split_axis=0, concat_axis=0, tiled=True)  30.5 us
    all_to_all x1, waiting for transfers between devices, body(): pieces = lax.all_to_all(pieces, EXP, split_axis=0, concat_axis=0)  28.7 us
  transfers between devices with their start and end apart: 8, of which 5 were waited for; matrix products, arithmetic and copies ran while one was open for 3% of the time, Pallas kernels for 0%

profile of v1, /device:TPU:8, one launch (start us, length us, event | category | flops | bytes accessed | tf_op | source)
XLA Modules:
  0.0 628.4 jit_solution(12841282803206582759)
XLA Ops:
  6.6 1.2 copy.84
  9.1 0.6 fusion.48
  9.8 1.0 copy.114
  11.5 0.7 copy-done.3
  12.3 1.5 convolution_convert_fusion.2
  13.8 4.3 all-to-all-start
  18.2 305.4 %all-gather.3 = f32[256,1,8]{2,1,0:T(1,128)S(1)} all-gather(f32[1,1,8]{2,1,0:T(1,128)S(1)} %get-tuple-element.21), channel_id=1, replica_groups=mesh['z'=16,'ylo'=2,'x'=4,'core'=2,'yhi'=2] {'z','ylo','x','core'}, dimensions={0}, use_global_device_ids=true | all-gather | bytes 8224 | tf_op jit(solution)/shard_map/all_gather | solution.py:33
  323.9 0.7 multiply_reduce_fusion.3
  324.7 0.7 all-gather.10.cloned.1.call-update
  325.9 0.9 copy.94
  326.9 0.6 reduce-window.6
  328.9 0.6 multiply_reduce_fusion
  329.7 125.3 %all-gather.8.cloned.1.call-done = bf16[4096,128]{1,0:T(8,128)(2,1)} async-done(((bf16[128,128]{1,0:T(8,128)(2,1)}), bf16[4096,128]{1,0:T(8,128)(2,1)}) %all-gather.8.cloned.1.call-update) | async-done | bytes 1048592 | tf_op jit(solution)/shard_map/all_gather | solution.py:44
  455.0 1.5 fusion.6
  456.6 0.8 add_convert_fusion
  457.5 4.2 all-to-all-start.1
  461.9 7.2 %all-to-all-done.1 = bf16[8,128,128]{1,2,0:T(8,128)(2,1)S(1)} async-done(((bf16[8,128,128]{1,2,0:T(8,128)(2,1)}), bf16[8,128,128]{1,2,0:T(8,128)(2,1)S(1)}, u32[]{:S(2)}, u32[]{:S(2)}) %all-to-all-start.1) | async-done | bytes 262176 | tf_op jit(solution)/shard_map/all_to_all | solution.py:12
  469.5 0.6 fusion.49
  471.1 1.1 reshape.256
  472.2 14.4 %all-to-all-start.2 = ((bf16[64,40,128]{2,1,0:T(8,128)(2,1)}), bf16[64,40,128]{2,1,0:T(8,128)(2,1)S(1)}, u32[]{:S(2)}, u32[]{:S(2)}) async-start(bf16[64,40,128]{2,1,0:T(8,128)(2,1)} %reshape.256), calls=%async_computation.2 | async-start | bytes 1310720 | tf_op jit(solution)/shard_map/all_to_all | solution.py:12
  486.6 0.7 all-gather.12.cloned.1.call-update
  487.3 37.6 %all-to-all-done.2 = bf16[64,40,128]{2,1,0:T(8,128)(2,1)S(1)} async-done(((bf16[64,40,128]{2,1,0:T(8,128)(2,1)}), bf16[64,40,128]{2,1,0:T(8,128)(2,1)S(1)}, u32[]{:S(2)}, u32[]{:S(2)}) %all-to-all-start.2) | async-done | bytes 655392 | tf_op jit(solution)/shard_map/all_to_all | solution.py:12
  524.9 1.8 stack.3
  526.7 3.8 all-to-all-start.3
  530.5 2.1 reshape.257
  532.6 4.5 fusion.1
  537.1 28.7 %all-to-all-done.3 = bf16[8,128,1408]{2,1,0:T(8,128)(2,1)S(1)} async-done(((bf16[8,128,1408]{2,1,0:T(8,128)(2,1)}), bf16[8,128,1408]{2,1,0:T(8,128)(2,1)S(1)}, u32[]{:S(2)}, u32[]{:S(2)}) %all-to-all-start.3) | async-done | bytes 2883616 | tf_op jit(solution)/shard_map/all_to_all | solution.py:149
  565.8 5.6 convolution_convert_fusion.1
  571.4 2.2 reshape.259
  573.6 7.7 %all-to-all-start.4 = ((bf16[64,40,128]{2,1,0:T(8,128)(2,1)}), bf16[64,40,128]{2,1,0:T(8,128)(2,1)S(1)}, u32[]{:S(2)}, u32[]{:S(2)}) async-start(bf16[64,40,128]{2,1,0:T(8,128)(2,1)} %reshape.259), calls=%async_computation.4 | async-start | bytes 1310720 | tf_op jit(solution)/shard_map/all_to_all | solution.py:12
  581.7 38.5 %all-to-all-done.4 = bf16[64,40,128]{2,1,0:T(8,128)(2,1)S(1)} async-done(((bf16[64,40,128]{2,1,0:T(8,128)(2,1)}), bf16[64,40,128]{2,1,0:T(8,128)(2,1)S(1)}, u32[]{:S(2)}, u32[]{:S(2)}) %all-to-all-start.4) | async-done | bytes 655392 | tf_op jit(solution)/shard_map/all_to_all | solution.py:12
  620.8 1.1 fusion.14
  (94 shorter events, 7.1 us)
Async XLA Ops:
  6.5 1.7 copy-start.8
  7.7 1.1 copy-start.11
  11.2 314.3 %copy-start.12 = (s32[1,128,2]{1,2,0:T(2,128)S(1)}, s32[1,128,2]{1,2,0:T(2,128)}, u32[]{:S(2)}) copy-start(s32[1,128,2]{1,2,0:T(2,128)} %param.19) | copy-start | bytes 3076
  11.5 0.7 copy-start.3
  11.5 0.8 copy-start.5
  13.8 310.1 %all-to-all-start = ((bf16[8,128,128]{2,1,0:T(8,128)(2,1)}), bf16[8,128,128]{2,1,0:T(8,128)(2,1)S(1)}, u32[]{:S(2)}, u32[]{:S(2)}) async-start(bf16[8,128,128]{2,1,0:T(8,128)(2,1)} %convolution_convert_fusion.2), calls=%async_computation | async-start | bytes 524288 | tf_op jit(solution)/shard_map/all_to_all | solution.py:12
  18.1 436.9 %all-gather.8.cloned.1.call-start = ((), (), s32[]{:S(2)}) async-start(), calls=%async_computation.5 | async-start | bytes 1081344 | tf_op jit(solution)/shard_map/all_gather | solution.py:44
  324.7 207.9 %all-gather.10.cloned.1.call-start = ((), (), s32[]{:S(2)}) async-start(), calls=%async_computation.6 | async-start | bytes 3244032 | tf_op jit(solution)/shard_map/all_gather | solution.py:144
  329.5 140.0 %copy-start.4 = (bf16[128,8,64]{2,0,1:T(8,128)(2,1)S(1)}, bf16[128,8,64]{2,0,1:T(8,128)(2,1)}, u32[]{:S(2)}) copy-start(bf16[128,8,64]{2,0,1:T(8,128)(2,1)} %copy-done.3) | copy-start | bytes 393220
  329.5 140.0 %copy-start.6 = (bf16[128,8,64]{2,0,1:T(8,128)(2,1)S(1)}, bf16[128,8,64]{2,0,1:T(8,128)(2,1)}, u32[]{:S(2)}) copy-start(bf16[128,8,64]{2,0,1:T(8,128)(2,1)} %copy-done.5) | copy-start | bytes 393220
  457.5 11.7 %all-to-all-start.1 = ((bf16[8,128,128]{1,2,0:T(8,128)(2,1)}), bf16[8,128,128]{1,2,0:T(8,128)(2,1)S(1)}, u32[]{:S(2)}, u32[]{:S(2)}) async-start(bf16[8,128,128]{1,2,0:T(8,128)(2,1)} %add_convert_fusion), calls=%async_computation.1 | async-start | bytes 524288 | tf_op jit(solution)/shard_map/all_to_all | solution.py:12
  461.9 8.6 %copy-start.1 = (bf16[1,128,1024]{2,1,0:T(8,128)(2,1)S(1)}, bf16[1,128,1024]{2,1,0:T(8,128)(2,1)}, u32[]{:S(2)}) copy-start(bf16[1,128,1024]{2,1,0:T(8,128)(2,1)} %param.12) | copy-start | bytes 786436
  461.9 8.6 %copy-start.9 = (f32[1024]{0:T(1024)S(1)}, f32[1024]{0:T(1024)}, u32[]{:S(2)}) copy-start(f32[1024]{0:T(1024)} %param.17) | copy-start | bytes 12292
  469.5 1.2 copy-start.10
  470.4 54.4 %copy-start.7 = (bf16[1,128,1408]{2,1,0:T(8,128)(2,1)S(1)}, bf16[1,128,1408]{2,1,0:T(8,128)(2,1)}, u32[]{:S(2)}) copy-start(bf16[1,128,1408]{2,1,0:T(8,128)(2,1)} %param.23) | copy-start | bytes 1081348
  472.2 52.7 %all-to-all-start.2 = ((bf16[64,40,128]{2,1,0:T(8,128)(2,1)}), bf16[64,40,128]{2,1,0:T(8,128)(2,1)S(1)}, u32[]{:S(2)}, u32[]{:S(2)}) async-start(bf16[64,40,128]{2,1,0:T(8,128)(2,1)} %reshape.256), calls=%async_computation.2 | async-start | bytes 1310720 | tf_op jit(solution)/shard_map/all_to_all | solution.py:12
  486.5 79.3 %all-gather.12.cloned.1.call-start = ((), (), s32[]{:S(2)}) async-start(), calls=%async_computation.7 | async-start | bytes 3244032 | tf_op jit(solution)/shard_map/all_gather | solution.py:145
  524.9 1.8 copy-start
  526.7 39.2 %all-to-all-start.3 = ((bf16[8,128,1408]{2,1,0:T(8,128)(2,1)}), bf16[8,128,1408]{2,1,0:T(8,128)(2,1)S(1)}, u32[]{:S(2)}, u32[]{:S(2)}) async-start(bf16[8,128,1408]{2,1,0:T(8,128)(2,1)} %stack.3), calls=%async_computation.3 | async-start | bytes 5767168 | tf_op jit(solution)/shard_map/all_to_all | solution.py:149
  571.4 10.2 %copy-start.13 = (f32[1,128,2]{1,2,0:T(2,128)S(1)}, f32[1,128,2]{1,2,0:T(2,128)}, u32[]{:S(2)}) copy-start(f32[1,128,2]{1,2,0:T(2,128)} %param.20) | copy-start | bytes 3076
  571.4 49.0 %copy-start.2 = (bf16[1,128,1024]{2,1,0:T(8,128)(2,1)S(1)}, bf16[1,128,1024]{2,1,0:T(8,128)(2,1)}, u32[]{:S(2)}) copy-start(bf16[1,128,1024]{2,1,0:T(8,128)(2,1)} %param.12) | copy-start | bytes 786436
  573.6 46.5 %all-to-all-start.4 = ((bf16[64,40,128]{2,1,0:T(8,128)(2,1)}), bf16[64,40,128]{2,1,0:T(8,128)(2,1)S(1)}, u32[]{:S(2)}, u32[]{:S(2)}) async-start(bf16[64,40,128]{2,1,0:T(8,128)(2,1)} %reshape.259), calls=%async_computation.4 | async-start | bytes 1310720 | tf_op jit(solution)/shard_map/all_to_all | solution.py:12
Sparse Core Ops, SparseCore 0:
  324.8 130.1 all-gather.7
  457.1 34.1 all-gather.9
  493.5 34.6 all-gather.11
